TPU v7x, 256 devices: a whole 4x4x8 slice. The times are simulated.
256 devices in a mesh: trow: 4 (over y), tcol: 4 (over x), pix: 16 (over z, core).
Axes of the slice: x: 4, y: 4, z: 8, core: 2. Of those that a mesh axis runs over, the one named last changes fastest.
Arguments:
- frames: float32 [6144, 2, 64, 128], P(('trow', 'tcol'), None, 'pix'), may hold values from 0.1 to 8
- drift: int32 [6144, 2], P(('trow', 'tcol')), may hold values from -7 to 7
Outputs:
- inner_cycle: float32 [6144, 6144], P(('trow', 'pix'), 'tcol')
- second_band_twotime: float32 [6144, 6144], P(('trow', 'pix'), 'tcol')
All inputs are finite; a program needn't handle non-finite values.
Results may differ from a plain program's by a relative error of at most 0.0003.
Values may be sent and summed in bfloat16 or wider, within the bound.
A program may use at most 128 MiB of HBM per device.

v0:
```python
import jax
import jax.numpy as jnp
from jax import lax
from jax.sharding import PartitionSpec as P


def extended(cells, sides, width):
    for axis, dim in sides:
        count = lax.axis_size(axis)
        ends = count - 1
        head = lax.slice_in_dim(cells, 0, width, axis=dim)
        tail = lax.slice_in_dim(cells, cells.shape[dim] - width, cells.shape[dim], axis=dim)
        cells = jnp.concatenate(
            [
                lax.ppermute(tail, axis, [(i, (i + 1) % count) for i in range(ends)]),
                cells,
                lax.ppermute(head, axis, [((i + 1) % count, i) for i in range(ends)]),
            ],
            axis=dim,
        )
    return cells


def blend(padded, steps, device_axis):
    upward = (jnp.maximum(steps, 0).astype(jnp.float32) / 8.0)[:, None, None, None]
    downward = (jnp.maximum(-steps, 0).astype(jnp.float32) / 8.0)[:, None, None, None]
    length = padded.shape[device_axis] - 2
    middle = lax.slice_in_dim(padded, 1, 1 + length, 1, device_axis)
    after = lax.slice_in_dim(padded, 2, 2 + length, 1, device_axis)
    before = lax.slice_in_dim(padded, 0, length, 1, device_axis)
    return (1.0 - upward - downward) * middle + upward * after + downward * before


def per_device(frames, drift):
    local_frames = frames.shape[0]
    tile_rows = frames.shape[2]
    columns = frames.shape[3]
    total_frames = local_frames * lax.axis_size("trow") * lax.axis_size("tcol")
    band_pixels = tile_rows * columns * lax.axis_size("pix")
    padded = extended(frames.astype(jnp.bfloat16), (("pix", 2),), 1).astype(frames.dtype)
    rowpass = blend(padded, drift[:, 0], 2)
    padded = jnp.pad(rowpass, ((0, 0), (0, 0), (0, 0), (1, 1)))
    shifted = blend(padded, drift[:, 1], 3)
    pixel_mean = lax.psum(jnp.sum(shifted, axis=0), ("trow", "tcol")) / total_frames
    flat = shifted / pixel_mean[None]
    frame_mean = lax.psum(jnp.sum(flat, axis=(2, 3)), "pix") / band_pixels
    normed = (flat / frame_mean[:, :, None, None]).astype(jnp.bfloat16)
    normed = normed.reshape(local_frames, 2, tile_rows * columns)
    block_size = local_frames * lax.axis_size("tcol")
    everything = lax.all_gather(normed, ("trow", "tcol"), axis=0, tiled=True)
    row_frames = lax.dynamic_slice_in_dim(
        everything, lax.axis_index("trow") * block_size, block_size, 0
    )
    col_frames = lax.dynamic_slice_in_dim(
        everything, lax.axis_index("tcol") * block_size, block_size, 0
    )
    own_rows = block_size // lax.axis_size("pix")
    results = []
    for band in range(2):
        band_rows = row_frames[:, band]
        band_cols = col_frames[:, band]

        def partial_gram(start, count, band_rows=band_rows, band_cols=band_cols):
            return lax.dot_general(
                band_rows, band_cols, (((1,), (1,)), ((), ())), preferred_element_type=jnp.float32
            )

        summed = lax.psum_scatter(
            partial_gram(jnp.int32(0), lax.axis_size("pix") * own_rows),
            "pix",
            scatter_dimension=0,
            tiled=True,
        )
        results.append(summed / band_pixels)
    return (results[0], results[1])


def solution(mesh):
    in_specs = (P(("trow", "tcol"), None, "pix", None), P(("trow", "tcol"), None))
    out_specs = (P(("trow", "pix"), "tcol"), P(("trow", "pix"), "tcol"))
    return jax.shard_map(
        per_device, mesh=mesh, in_specs=in_specs, out_specs=out_specs, check_vma=False
    )
```

profile of v0, /device:TPU:6, one launch (start us, length us, event | category | flops | bytes accessed | tf_op | source)
XLA Modules:
  0.0 343.2 jit_solution(5031230959455782191)
XLA Ops:
  7.2 0.0 copy-start
  7.2 0.0 all-gather.2.cloned.1.call-start
  7.2 1.7 copy.10
  9.0 1.8 collective-permute-start
  10.7 1.3 collective-permute-start.1
  12.0 0.0 copy-done
  12.1 0.0 collective-permute-done
  12.1 3.7 %collective-permute-done.1 = bf16[384,2,1,128]{3,0,2,1:T(8,128)(2,1)S(1)} collective-permute-done((bf16[384,2,1,128]{3,0,2,1:T(8,128)(2,1)S(1)}, bf16[384,2,1,128]{3,0,2,1:T(8,128)(2,1)S(1)}, u32[]{:S(2)}, u32[]{:S(2)}) %collective-permute-start.1) | collective-permute-done | bytes 196640 | tf_op jit(solution)/shard_map/ppermute | solution.py:17
  15.8 0.2 maximum_convert_fusion
  15.9 0.4 fusion.6
  16.3 1.0 fusion.11
  17.4 32.7 %psum.14 = f32[2,4,128]{2,1,0:T(4,128)S(1)} all-reduce(f32[2,4,128]{2,1,0:T(4,128)S(1)} %get-tuple-element.6), channel_id=1, replica_groups=mesh['trow'=4,'tcol'=4,'pix'=16] {'trow','tcol'}, use_global_device_ids=true, to_apply=%region_1.2 | all-reduce | flops 1024 | bytes 8192 | tf_op jit(solution)/shard_map/psum | solution.py:44
  50.1 0.2 divide_reduce_fusion
  50.3 28.0 %psum.15 = f32[384,2]{0,1:T(2,128)S(1)} all-reduce(f32[384,2]{0,1:T(2,128)S(1)} %divide_reduce_fusion), channel_id=1, replica_groups=mesh['trow'=4,'tcol'=4,'pix'=16] {'pix'}, use_global_device_ids=true, to_apply=%region_3.4 | all-reduce | flops 768 | bytes 6144 | tf_op jit(solution)/shard_map/psum | solution.py:46
  78.3 1.2 copy_bitcast_fusion
  79.5 0.0 all-gather.2.cloned.1.call-update
  79.5 0.0 reduce-scatter.5.cloned.1.call-start
  79.6 99.5 %all-gather.2.cloned.1.call-done = bf16[6144,2,512]{2,0,1:T(8,128)(2,1)} async-done(((bf16[384,2,512]{2,0,1:T(8,128)(2,1)}), bf16[6144,2,512]{2,0,1:T(8,128)(2,1)}) %all-gather.2.cloned.1.call-update) | async-done | bytes 12582928 | tf_op jit(solution)/shard_map/all_gather | solution.py:50
  179.1 8.2 %fusion.4 = f32[1536,1536]{1,0:T(8,128)} fusion(bf16[6144,2,512]{2,0,1:T(8,128)(2,1)} %all-gather.2.cloned.1.call-done, s32[]{:T(128)S(6)} %select_n.7, s32[]{:T(128)S(6)} %add.38, s32[]{:T(128)S(6)} %select_n.6), kind=kOutput, calls=%fused_computation.7 | convolution fusion | flops 2415919104 | bytes 12584960 | tf_op jit(solution)/shard_map/dot_general | solution.py:64
  187.3 0.0 reduce-scatter.5.cloned.1.call-update
  187.3 0.0 reduce-scatter.3.cloned.1.call-start
  187.4 8.1 %fusion.5 = f32[1536,1536]{1,0:T(8,128)} fusion(bf16[6144,2,512]{2,0,1:T(8,128)(2,1)} %all-gather.2.cloned.1.call-done, s32[]{:T(128)S(6)} %select_n.7, s32[]{:T(128)S(6)} %select_n.6), kind=kOutput, calls=%fused_computation.10 | convolution fusion | flops 2415919104 | bytes 12582920 | tf_op jit(solution)/shard_map/dot_general | solution.py:64
  195.5 0.0 reduce-scatter.3.cloned.1.call-update
  195.5 64.3 %reduce-scatter.5.cloned.1.call-done = f32[96,1536]{1,0:T(8,128)} async-done(((f32[1536,1536]{1,0:T(8,128)}), f32[96,1536]{1,0:T(8,128)}) %reduce-scatter.5.cloned.1.call-update) | async-done | bytes 589840 | tf_op jit(solution)/shard_map/reduce_scatter | solution.py:68
  259.8 1.9 broadcast_multiply_fusion
  261.7 73.0 %reduce-scatter.3.cloned.1.call-done = f32[96,1536]{1,0:T(8,128)} async-done(((f32[1536,1536]{1,0:T(8,128)}), f32[96,1536]{1,0:T(8,128)}) %reduce-scatter.3.cloned.1.call-update) | async-done | bytes 589840 | tf_op jit(solution)/shard_map/reduce_scatter | solution.py:68
  334.7 1.9 broadcast_multiply_fusion.1
  (5 shorter events, 0.1 us)
Async XLA Ops:
  7.2 4.9 %copy-start = (s32[384,2]{0,1:T(2,128)S(1)}, s32[384,2]{0,1:T(2,128)}, u32[]{:S(2)}) copy-start(s32[384,2]{0,1:T(2,128)} %param.3) | copy-start | bytes 9220
  7.2 172.0 %all-gather.2.cloned.1.call-start = ((), (), s32[]{:S(2)}) async-start(), calls=%async_computation.2 | async-start | bytes 13369344 | tf_op jit(solution)/shard_map/all_gather | solution.py:50
  9.0 3.1 collective-permute-start
  10.7 5.0 %collective-permute-start.1 = (bf16[384,2,1,128]{3,0,2,1:T(8,128)(2,1)S(1)}, bf16[384,2,1,128]{3,0,2,1:T(8,128)(2,1)S(1)}, u32[]{:S(2)}, u32[]{:S(2)}) collective-permute-start(bf16[384,2,1,128]{3,0,2,1:T(8,128)(2,1)S(1)} %get-tuple-element.9), channel_id=1, source_target_pairs={{1,0},{2,1},{3,2},{4,3},{5,4},{6,5},{7,6},{8,7},{9,8},{10,9},{11,1... | collective-permute-start | bytes 589832 | tf_op jit(solution)/shard_map/ppermute | solution.py:17
  79.5 180.3 %reduce-scatter.5.cloned.1.call-start = ((), (), s32[]{:S(2)}) async-start(), calls=%async_computation.4 | async-start | bytes 10027008 | tf_op jit(solution)/shard_map/reduce_scatter | solution.py:68
  187.3 147.4 %reduce-scatter.3.cloned.1.call-start = ((), (), s32[]{:S(2)}) async-start(), calls=%async_computation.3 | async-start | bytes 10027008 | tf_op jit(solution)/shard_map/reduce_scatter | solution.py:68
Sparse Core Ops, SparseCore 0:
  79.7 99.4 all-gather.1
  187.5 72.3 reduce-scatter.4
  262.4 72.2 reduce-scatter.2
where the time goes:
time: 343 us
  waiting for transfers between devices  240 us (70%)
  blocking collectives  60.7 us (18%)
  matrix products  16.3 us (5%)
  between operations  13.8 us (4%)
  other arithmetic  6.9 us (2%)
    reduce_scatter x2, waiting for transfers between devices, per_device(): lax.psum_scatter(partial_gram(jnp.int32(0), lax.axis_size('pix') * own_ro...  137 us
    all_gather x1, waiting for transfers between devices, per_device(): everything = lax.all_gather(normed, ('trow', 'tcol'), axis=0, tiled=True)  99.5 us
    psum x1, blocking collectives, per_device(): lax.psum(jnp.sum(shifted, axis=0), ('trow', 'tcol')) / total_frames  32.7 us
    psum x1, blocking collectives, per_device(): frame_mean = lax.psum(jnp.sum(flat, axis=(2, 3)), 'pix') / band_pixels  28 us
    dot_general x2, matrix products, partial_gram(): lax.dot_general(band_rows, band_cols, (((1,), (1,)), ((), ())), preferred...  16.3 us
  transfers between devices with their start and end apart: 5, of which 4 were waited for; matrix products, arithmetic and copies ran while one was open for 3% of the time, Pallas kernels for 0%

commit v1 on v0

--- a/solution.py
+++ b/solution.py
@@ -2,6 +2,38 @@
 import jax.numpy as jnp
 from jax import lax
 from jax.sharding import PartitionSpec as P
+
+
+def finish_cycles(block_in, group_axis):
+    work_now, kept_arr, u1 = (
+        lax.psum(1, axis_name=group_axis),
+        lax.axis_index(group_axis),
+        block_in.shape[0],
+    )
+    slots = [idx * work_now if j == 0 else idx for j, idx in enumerate(block_in.shape)]
+    clean = value_now = block_in
+    mixed_arr = lax.dynamic_update_slice_in_dim(
+        jnp.zeros(slots, block_in.dtype), block_in, kept_arr * u1, axis=0
+    )
+    for tick in range(1, work_now // 2 + 1):
+        clean = lax.ppermute(
+            clean,
+            axis_name=group_axis,
+            perm=list(map(lambda j: (j, (j + 1) % work_now), range(work_now))),
+        )
+        mixed_arr = lax.dynamic_update_slice_in_dim(
+            mixed_arr, clean, (kept_arr - tick) % work_now * u1, axis=0
+        )
+        if 2 * tick < work_now:
+            value_now = lax.ppermute(
+                value_now,
+                axis_name=group_axis,
+                perm=list(map(lambda j: (j, (j - 1) % work_now), range(work_now))),
+            )
+            mixed_arr = lax.dynamic_update_slice_in_dim(
+                mixed_arr, value_now, (kept_arr + tick) % work_now * u1, axis=0
+            )
+    return mixed_arr
 
 
 def extended(cells, sides, width):
@@ -47,7 +79,7 @@
     normed = (flat / frame_mean[:, :, None, None]).astype(jnp.bfloat16)
     normed = normed.reshape(local_frames, 2, tile_rows * columns)
     block_size = local_frames * lax.axis_size("tcol")
-    everything = lax.all_gather(normed, ("trow", "tcol"), axis=0, tiled=True)
+    everything = finish_cycles(normed, ("trow", "tcol"))
     row_frames = lax.dynamic_slice_in_dim(
         everything, lax.axis_index("trow") * block_size, block_size, 0
     )

time: 343 us -> 409 us (1.19)
  starting transfers between devices: 3.16 us -> 35.6 us
  local copies, waits for them, and re-layouts: 1.75 us -> 25.9 us
  waiting for transfers between devices: 240 us -> 245 us
    ppermute x0 -> x15, waiting for transfers between devices: none -> 101 us  [the longest x8 98.1 us: finish_cycles(): lax.ppermute(clean, axis_name=group_axis, perm=list(map(lambda j: (j, (j...]
    all_gather x1 -> x0, waiting for transfers between devices: 99.5 us -> none  [per_device(): everything = lax.all_gather(normed, ('trow', 'tcol'), axis=0, tiled=True)]
    ppermute x0 -> x15, starting transfers between devices: none -> 31.2 us  [the longest x8 19.8 us: finish_cycles(): lax.ppermute(clean, axis_name=group_axis, perm=list(map(lambda j: (j, (j...]
    dynamic_update_slice x0 -> x15, local copies, waits for them, and re-layouts: none -> 18.8 us  [the longest x8 9.89 us: finish_cycles(): lax.dynamic_update_slice_in_dim(mixed_arr, clean, (kept_arr - tick) % wor...]
    reduce_scatter x2, waiting for transfers between devices: 137 us -> 145 us  [per_device(): lax.psum_scatter(partial_gram(jnp.int32(0), lax.axis_size('pix') * own_ro...]
    broadcast_in_dim x0 -> x1, local copies, waits for them, and re-layouts: none -> 5.34 us  [finish_cycles(): jnp.zeros(slots, block_in.dtype)]
  transfers between devices with their start and end apart: 5 -> 19, of which waited for: 4 -> 12; matrix products, arithmetic and copies ran while one was open for 3% -> 9% of each run, Pallas kernels for 0% -> 0%
where the time goes in v1:
time: 409 us; the launch traced here: 408 us
  waiting for transfers between devices  245 us (60%)
  blocking collectives  62.7 us (15%)
  starting transfers between devices  35.6 us (9%)
  local copies, waits for them, and re-layouts  25.9 us (6%)
  matrix products  16.3 us (4%)
  between operations  14.1 us (3%)
  other arithmetic  7.91 us (2%)
    reduce_scatter x2, waiting for transfers between devices, per_device(): lax.psum_scatter(partial_gram(jnp.int32(0), lax.axis_size('pix') * own_ro...  145 us
    ppermute x8, waiting for transfers between devices, finish_cycles(): lax.ppermute(clean, axis_name=group_axis, perm=list(map(lambda j: (j, (j...  98.1 us
    psum x1, blocking collectives, per_device(): lax.psum(jnp.sum(shifted, axis=0), ('trow', 'tcol')) / total_frames  33.7 us
    psum x1, blocking collectives, per_device(): frame_mean = lax.psum(jnp.sum(flat, axis=(2, 3)), 'pix') / band_pixels  29 us
    ppermute x8, starting transfers between devices, finish_cycles(): lax.ppermute(clean, axis_name=group_axis, perm=list(map(lambda j: (j, (j...  19.8 us
    dot_general x2, matrix products, partial_gram(): lax.dot_general(band_rows, band_cols, (((1,), (1,)), ((), ())), preferred...  16.3 us
    ppermute x7, starting transfers between devices, finish_cycles(): lax.ppermute(value_now, axis_name=group_axis, perm=list(map(lambda j: (j,...  11.4 us
    dynamic_update_slice x8, local copies, waits for them, and re-layouts, finish_cycles(): lax.dynamic_update_slice_in_dim(mixed_arr, clean, (kept_arr - tick) % wor...  9.89 us
  transfers between devices with their start and end apart: 19, of which 12 were waited for; matrix products, arithmetic and copies ran while one was open for 9% of the time, Pallas kernels for 0%

profile of v1, /device:TPU:6, one launch (start us, length us, event | category | flops | bytes accessed | tf_op | source)
XLA Modules:
  0.0 408.0 jit_solution(16572981332965644357)
XLA Ops:
  7.2 1.7 copy.12
  9.0 1.3 collective-permute-start.1
  10.3 3.0 collective-permute-start
  14.9 1.0 fusion.11
  16.0 33.7 %psum.14 = f32[2,4,128]{2,1,0:T(4,128)S(1)} all-reduce(f32[2,4,128]{2,1,0:T(4,128)S(1)} %get-tuple-element.6), channel_id=1, replica_groups=mesh['trow'=4,'tcol'=4,'pix'=16] {'trow','tcol'}, use_global_device_ids=true, to_apply=%region_1.2 | all-reduce | flops 1024 | bytes 8192 | tf_op jit(solution)/shard_map/psum | solution.py:76
  49.9 29.0 %psum.15 = f32[384,2]{0,1:T(2,128)S(1)} all-reduce(f32[384,2]{0,1:T(2,128)S(1)} %divide_reduce_fusion), channel_id=1, replica_groups=mesh['trow'=4,'tcol'=4,'pix'=16] {'pix'}, use_global_device_ids=true, to_apply=%region_3.4 | all-reduce | flops 768 | bytes 6144 | tf_op jit(solution)/shard_map/psum | solution.py:78
  79.2 3.4 collective-permute-start.2
  82.6 1.3 collective-permute-start.3
  83.9 18.0 %collective-permute-done.2 = bf16[384,2,512]{2,0,1:T(8,128)(2,1)S(1)} collective-permute-done((bf16[384,2,512]{2,0,1:T(8,128)(2,1)S(1)}, bf16[384,2,512]{2,0,1:T(8,128)(2,1)S(1)}, u32[]{:S(2)}, u32[]{:S(2)}) %collective-permute-start.2) | collective-permute-done | bytes 786464 | tf_op jit(solution)/shard_map/ppermute | solution.py:19
  101.8 2.6 collective-permute-start.4
  104.5 16.7 %collective-permute-done.4 = bf16[384,2,512]{2,0,1:T(8,128)(2,1)S(1)} collective-permute-done((bf16[384,2,512]{2,0,1:T(8,128)(2,1)S(1)}, bf16[384,2,512]{2,0,1:T(8,128)(2,1)S(1)}, u32[]{:S(2)}, u32[]{:S(2)}) %collective-permute-start.4) | collective-permute-done | bytes 786464 | tf_op jit(solution)/shard_map/ppermute | solution.py:19
  121.1 4.4 %collective-permute-start.6 = (bf16[384,2,512]{2,0,1:T(8,128)(2,1)S(1)}, bf16[384,2,512]{2,0,1:T(8,128)(2,1)S(1)}, u32[]{:S(2)}, u32[]{:S(2)}) collective-permute-start(bf16[384,2,512]{2,0,1:T(8,128)(2,1)S(1)} %collective-permute-done.4), channel_id=1, source_target_pairs={{0,16},{16,32},{32,48},{48,64},{64,80},{80,96},{96,112},{112,128},... | collective-permute-start | bytes 2359304 | tf_op jit(solution)/shard_map/ppermute | solution.py:19
  125.6 16.2 %collective-permute-done.6 = bf16[384,2,512]{2,0,1:T(8,128)(2,1)S(1)} collective-permute-done((bf16[384,2,512]{2,0,1:T(8,128)(2,1)S(1)}, bf16[384,2,512]{2,0,1:T(8,128)(2,1)S(1)}, u32[]{:S(2)}, u32[]{:S(2)}) %collective-permute-start.6) | collective-permute-done | bytes 786464 | tf_op jit(solution)/shard_map/ppermute | solution.py:19
  141.8 4.0 collective-permute-start.8
  145.8 1.3 collective-permute-start.9
  147.0 15.1 %collective-permute-done.8 = bf16[384,2,512]{2,0,1:T(8,128)(2,1)S(1)} collective-permute-done((bf16[384,2,512]{2,0,1:T(8,128)(2,1)S(1)}, bf16[384,2,512]{2,0,1:T(8,128)(2,1)S(1)}, u32[]{:S(2)}, u32[]{:S(2)}) %collective-permute-start.8) | collective-permute-done | bytes 786464 | tf_op jit(solution)/shard_map/ppermute | solution.py:19
  162.2 2.9 collective-permute-start.10
  165.0 2.5 collective-permute-start.11
  167.5 14.4 %collective-permute-done.10 = bf16[384,2,512]{2,0,1:T(8,128)(2,1)} collective-permute-done((bf16[384,2,512]{2,0,1:T(8,128)(2,1)S(1)}, bf16[384,2,512]{2,0,1:T(8,128)(2,1)}, u32[]{:S(2)}, u32[]{:S(2)}) %collective-permute-start.10) | collective-permute-done | bytes 786464 | tf_op jit(solution)/shard_map/ppermute | solution.py:19
  181.8 1.6 collective-permute-start.12
  183.5 5.3 %broadcast_in_dim.2 = bf16[6144,2,512]{2,0,1:T(8,128)(2,1)} broadcast(bf16[]{:T(256)} %constant.110.clone.1), dimensions={} | broadcast | bytes 12582914 | tf_op jit(solution)/shard_map/broadcast_in_dim | solution.py:16
  188.8 1.2 constant_dynamic-update-slice_fusion.15
  190.0 1.0 constant_dynamic-update-slice_fusion.14
  191.0 2.9 collective-permute-start.13
  193.9 1.0 constant_dynamic-update-slice_fusion.13
  194.8 6.0 %collective-permute-done.12 = bf16[384,2,512]{2,0,1:T(8,128)(2,1)} collective-permute-done((bf16[384,2,512]{2,0,1:T(8,128)(2,1)}, bf16[384,2,512]{2,0,1:T(8,128)(2,1)}, u32[]{:S(2)}, u32[]{:S(2)}) %collective-permute-start.12) | collective-permute-done | bytes 786464 | tf_op jit(solution)/shard_map/ppermute | solution.py:19
  201.2 1.0 constant_dynamic-update-slice_fusion.12
  202.2 1.0 constant_dynamic-update-slice_fusion.11
  203.1 1.0 constant_dynamic-update-slice_fusion.10
  204.1 1.0 constant_dynamic-update-slice_fusion.9
  205.1 0.9 constant_dynamic-update-slice_fusion.8
  206.0 2.5 collective-permute-done.13
  208.6 3.4 collective-permute-start.15
  212.0 2.1 constant_dynamic-update-slice_fusion.7
  214.1 4.5 %collective-permute-done.14 = bf16[384,2,512]{2,0,1:T(8,128)(2,1)S(1)} collective-permute-done((bf16[384,2,512]{2,0,1:T(8,128)(2,1)}, bf16[384,2,512]{2,0,1:T(8,128)(2,1)S(1)}, u32[]{:S(2)}, u32[]{:S(2)}) %collective-permute-start.14) | collective-permute-done | bytes 786464 | tf_op jit(solution)/shard_map/ppermute | solution.py:19
  219.1 2.1 constant_dynamic-update-slice_fusion.6
  221.2 2.1 constant_dynamic-update-slice_fusion.5
  223.3 2.1 constant_dynamic-update-slice_fusion.4
  226.3 0.9 constant_dynamic-update-slice_fusion.2
  227.2 0.9 constant_dynamic-update-slice_fusion.1
  228.2 7.3 %collective-permute-done.16 = bf16[384,2,512]{2,0,1:T(8,128)(2,1)S(1)} collective-permute-done((bf16[384,2,512]{2,0,1:T(8,128)(2,1)S(1)}, bf16[384,2,512]{2,0,1:T(8,128)(2,1)S(1)}, u32[]{:S(2)}, u32[]{:S(2)}) %collective-permute-start.16) | collective-permute-done | bytes 786464 | tf_op jit(solution)/shard_map/ppermute | solution.py:19
  235.4 1.0 constant_dynamic-update-slice_fusion
  236.4 8.1 %fusion.5 = f32[1536,1536]{1,0:T(8,128)} fusion(bf16[6144,2,512]{2,0,1:T(8,128)(2,1)} %constant_dynamic-update-slice_fusion, s32[]{:T(128)S(6)} %select_n.149, s32[]{:T(128)S(6)} %select_n.148), kind=kOutput, calls=%fused_computation.10 | convolution fusion | flops 2415919104 | bytes 12582920 | tf_op jit(solution)/shard_map/dot_general | solution.py:96
  244.6 8.2 %fusion.4 = f32[1536,1536]{1,0:T(8,128)} fusion(bf16[6144,2,512]{2,0,1:T(8,128)(2,1)} %constant_dynamic-update-slice_fusion, s32[]{:T(128)S(6)} %select_n.149, s32[]{:T(128)S(6)} %add.203, s32[]{:T(128)S(6)} %select_n.148), kind=kOutput, calls=%fused_computation.7 | convolution fusion | flops 2415919104 | bytes 12584960 | tf_op jit(solution)/shard_map/dot_general | solution.py:96
  252.8 72.0 %reduce-scatter.3.cloned.1.call-done = f32[96,1536]{1,0:T(8,128)} async-done(((f32[1536,1536]{1,0:T(8,128)}), f32[96,1536]{1,0:T(8,128)}) %reduce-scatter.3.cloned.1.call-update) | async-done | bytes 589840 | tf_op jit(solution)/shard_map/reduce_scatter | solution.py:100
  324.7 1.9 broadcast_multiply_fusion.1
  326.6 72.6 %reduce-scatter.5.cloned.1.call-done = f32[96,1536]{1,0:T(8,128)} async-done(((f32[1536,1536]{1,0:T(8,128)}), f32[96,1536]{1,0:T(8,128)}) %reduce-scatter.5.cloned.1.call-update) | async-done | bytes 589840 | tf_op jit(solution)/shard_map/reduce_scatter | solution.py:100
  399.3 1.9 broadcast_multiply_fusion
  (46 shorter events, 4.0 us)
Async XLA Ops:
  7.2 317.5 %reduce-scatter.3.cloned.1.call-start = ((), (), s32[]{:S(2)}) async-start(), calls=%async_computation.2 | async-start | bytes 10027008 | tf_op jit(solution)/shard_map/reduce_scatter | solution.py:100
  9.0 5.2 %collective-permute-start.1 = (bf16[384,2,1,128]{3,0,2,1:T(8,128)(2,1)S(1)}, bf16[384,2,1,128]{3,0,2,1:T(8,128)(2,1)S(1)}, u32[]{:S(2)}, u32[]{:S(2)}) collective-permute-start(bf16[384,2,1,128]{3,0,2,1:T(8,128)(2,1)S(1)} %get-tuple-element.9), channel_id=1, source_target_pairs={{1,0},{2,1},{3,2},{4,3},{5,4},{6,5},{7,6},{8,7},{9,8},{10,9},{11,1... | collective-permute-start | bytes 589832 | tf_op jit(solution)/shard_map/ppermute | solution.py:49
  10.3 4.1 %collective-permute-start = (bf16[384,2,1,128]{3,0,2,1:T(8,128)(2,1)S(1)}, bf16[384,2,1,128]{3,0,2,1:T(8,128)(2,1)S(1)}, u32[]{:S(2)}, u32[]{:S(2)}) collective-permute-start(bf16[384,2,1,128]{3,0,2,1:T(8,128)(2,1)S(1)} %get-tuple-element.8), channel_id=1, source_target_pairs={{0,1},{1,2},{2,3},{3,4},{4,5},{5,6},{6,7},{7,8},{8,9},{9,10},{10,1... | collective-permute-start | bytes 589832 | tf_op jit(solution)/shard_map/ppermute | solution.py:47
  79.2 22.6 %collective-permute-start.2 = (bf16[384,2,512]{2,0,1:T(8,128)(2,1)S(1)}, bf16[384,2,512]{2,0,1:T(8,128)(2,1)S(1)}, u32[]{:S(2)}, u32[]{:S(2)}) collective-permute-start(bf16[384,2,512]{2,0,1:T(8,128)(2,1)S(1)} %copy_bitcast_fusion), channel_id=1, source_target_pairs={{0,16},{16,32},{32,48},{48,64},{64,80},{80,96},{96,112},{112,128},... | collective-permute-start | bytes 2359304 | tf_op jit(solution)/shard_map/ppermute | solution.py:19
  82.6 21.9 %collective-permute-start.3 = (bf16[384,2,512]{2,0,1:T(8,128)(2,1)S(1)}, bf16[384,2,512]{2,0,1:T(8,128)(2,1)S(1)}, u32[]{:S(2)}, u32[]{:S(2)}) collective-permute-start(bf16[384,2,512]{2,0,1:T(8,128)(2,1)S(1)} %copy_bitcast_fusion), channel_id=1, source_target_pairs={{0,240},{16,0},{32,16},{48,32},{64,48},{80,64},{96,80},{112,96},{1... | collective-permute-start | bytes 2359304 | tf_op jit(solution)/shard_map/ppermute | solution.py:28
  101.8 2.6 copy-start.6
  101.8 19.3 %collective-permute-start.4 = (bf16[384,2,512]{2,0,1:T(8,128)(2,1)S(1)}, bf16[384,2,512]{2,0,1:T(8,128)(2,1)S(1)}, u32[]{:S(2)}, u32[]{:S(2)}) collective-permute-start(bf16[384,2,512]{2,0,1:T(8,128)(2,1)S(1)} %collective-permute-done.2), channel_id=1, source_target_pairs={{0,16},{16,32},{32,48},{48,64},{64,80},{80,96},{96,112},{112,128},... | collective-permute-start | bytes 2359304 | tf_op jit(solution)/shard_map/ppermute | solution.py:19
  104.5 21.1 %collective-permute-start.5 = (bf16[384,2,512]{2,0,1:T(8,128)(2,1)S(1)}, bf16[384,2,512]{2,0,1:T(8,128)(2,1)S(1)}, u32[]{:S(2)}, u32[]{:S(2)}) collective-permute-start(bf16[384,2,512]{2,0,1:T(8,128)(2,1)S(1)} %collective-permute-done.3), channel_id=1, source_target_pairs={{0,240},{16,0},{32,16},{48,32},{64,48},{80,64},{96,80},{112,96},{1... | collective-permute-start | bytes 2359304 | tf_op jit(solution)/shard_map/ppermute | solution.py:28
  121.1 20.6 %collective-permute-start.6 = (bf16[384,2,512]{2,0,1:T(8,128)(2,1)S(1)}, bf16[384,2,512]{2,0,1:T(8,128)(2,1)S(1)}, u32[]{:S(2)}, u32[]{:S(2)}) collective-permute-start(bf16[384,2,512]{2,0,1:T(8,128)(2,1)S(1)} %collective-permute-done.4), channel_id=1, source_target_pairs={{0,16},{16,32},{32,48},{48,64},{64,80},{80,96},{96,112},{112,128},... | collective-permute-start | bytes 2359304 | tf_op jit(solution)/shard_map/ppermute | solution.py:19
  125.6 16.2 %copy-start = (bf16[384,2,512]{2,0,1:T(8,128)(2,1)}, bf16[384,2,512]{2,0,1:T(8,128)(2,1)S(1)}, u32[]{:S(2)}) copy-start(bf16[384,2,512]{2,0,1:T(8,128)(2,1)S(1)} %collective-permute-done.5) | copy-start | bytes 2359300
  125.6 20.2 %collective-permute-start.7 = (bf16[384,2,512]{2,0,1:T(8,128)(2,1)S(1)}, bf16[384,2,512]{2,0,1:T(8,128)(2,1)S(1)}, u32[]{:S(2)}, u32[]{:S(2)}) collective-permute-start(bf16[384,2,512]{2,0,1:T(8,128)(2,1)S(1)} %collective-permute-done.5), channel_id=1, source_target_pairs={{0,240},{16,0},{32,16},{48,32},{64,48},{80,64},{96,80},{112,96},{1... | collective-permute-start | bytes 2359304 | tf_op jit(solution)/shard_map/ppermute | solution.py:28
  141.8 4.0 copy-start.2
  141.8 20.4 %collective-permute-start.8 = (bf16[384,2,512]{2,0,1:T(8,128)(2,1)S(1)}, bf16[384,2,512]{2,0,1:T(8,128)(2,1)S(1)}, u32[]{:S(2)}, u32[]{:S(2)}) collective-permute-start(bf16[384,2,512]{2,0,1:T(8,128)(2,1)S(1)} %collective-permute-done.6), channel_id=1, source_target_pairs={{0,16},{16,32},{32,48},{48,64},{64,80},{80,96},{96,112},{112,128},... | collective-permute-start | bytes 2359304 | tf_op jit(solution)/shard_map/ppermute | solution.py:19
  145.8 16.4 %copy-start.4 = (bf16[384,2,512]{2,0,1:T(8,128)(2,1)}, bf16[384,2,512]{2,0,1:T(8,128)(2,1)S(1)}, u32[]{:S(2)}) copy-start(bf16[384,2,512]{2,0,1:T(8,128)(2,1)S(1)} %collective-permute-done.7) | copy-start | bytes 2359300
  145.8 19.3 %collective-permute-start.9 = (bf16[384,2,512]{2,0,1:T(8,128)(2,1)S(1)}, bf16[384,2,512]{2,0,1:T(8,128)(2,1)}, u32[]{:S(2)}, u32[]{:S(2)}) collective-permute-start(bf16[384,2,512]{2,0,1:T(8,128)(2,1)S(1)} %collective-permute-done.7), channel_id=1, source_target_pairs={{0,240},{16,0},{32,16},{48,32},{64,48},{80,64},{96,80},{112,96},{1... | collective-permute-start | bytes 2359304 | tf_op jit(solution)/shard_map/ppermute | solution.py:28
  162.2 2.9 copy-start.8
  162.2 19.7 %collective-permute-start.10 = (bf16[384,2,512]{2,0,1:T(8,128)(2,1)S(1)}, bf16[384,2,512]{2,0,1:T(8,128)(2,1)}, u32[]{:S(2)}, u32[]{:S(2)}) collective-permute-start(bf16[384,2,512]{2,0,1:T(8,128)(2,1)S(1)} %collective-permute-done.8), channel_id=1, source_target_pairs={{0,16},{16,32},{32,48},{48,64},{64,80},{80,96},{96,112},{112,128},... | collective-permute-start | bytes 2359304 | tf_op jit(solution)/shard_map/ppermute | solution.py:19
  165.0 25.9 %collective-permute-start.11 = (bf16[384,2,512]{2,0,1:T(8,128)(2,1)}, bf16[384,2,512]{2,0,1:T(8,128)(2,1)}, u32[]{:S(2)}, u32[]{:S(2)}) collective-permute-start(bf16[384,2,512]{2,0,1:T(8,128)(2,1)} %collective-permute-done.9), channel_id=1, source_target_pairs={{0,240},{16,0},{32,16},{48,32},{64,48},{80,64},{96,80},{112,96},{1... | collective-permute-start | bytes 2359304 | tf_op jit(solution)/shard_map/ppermute | solution.py:28
  181.8 19.0 %collective-permute-start.12 = (bf16[384,2,512]{2,0,1:T(8,128)(2,1)}, bf16[384,2,512]{2,0,1:T(8,128)(2,1)}, u32[]{:S(2)}, u32[]{:S(2)}) collective-permute-start(bf16[384,2,512]{2,0,1:T(8,128)(2,1)} %collective-permute-done.10), channel_id=1, source_target_pairs={{0,16},{16,32},{32,48},{48,64},{64,80},{80,96},{96,112},{112,128},... | collective-permute-start | bytes 2359304 | tf_op jit(solution)/shard_map/ppermute | solution.py:19
  183.5 6.5 %copy-start.7 = (bf16[384,2,512]{2,0,1:T(8,128)(2,1)S(1)}, bf16[384,2,512]{2,0,1:T(8,128)(2,1)}, u32[]{:S(2)}) copy-start(bf16[384,2,512]{2,0,1:T(8,128)(2,1)} %copy-done.6) | copy-start | bytes 2359300
  183.5 18.7 %copy-start.1 = (bf16[384,2,512]{2,0,1:T(8,128)(2,1)S(1)}, bf16[384,2,512]{2,0,1:T(8,128)(2,1)}, u32[]{:S(2)}) copy-start(bf16[384,2,512]{2,0,1:T(8,128)(2,1)} %copy-done) | copy-start | bytes 2359300
  183.5 19.7 %copy-start.3 = (bf16[384,2,512]{2,0,1:T(8,128)(2,1)S(1)}, bf16[384,2,512]{2,0,1:T(8,128)(2,1)}, u32[]{:S(2)}) copy-start(bf16[384,2,512]{2,0,1:T(8,128)(2,1)} %copy-done.2) | copy-start | bytes 2359300
  183.5 20.6 %copy-start.5 = (bf16[384,2,512]{2,0,1:T(8,128)(2,1)S(1)}, bf16[384,2,512]{2,0,1:T(8,128)(2,1)}, u32[]{:S(2)}) copy-start(bf16[384,2,512]{2,0,1:T(8,128)(2,1)} %copy-done.4) | copy-start | bytes 2359300
  188.8 16.2 %copy-start.9 = (bf16[384,2,512]{2,0,1:T(8,128)(2,1)S(1)}, bf16[384,2,512]{2,0,1:T(8,128)(2,1)}, u32[]{:S(2)}) copy-start(bf16[384,2,512]{2,0,1:T(8,128)(2,1)} %copy-done.8) | copy-start | bytes 2359300
  191.0 17.6 %collective-permute-start.13 = (bf16[384,2,512]{2,0,1:T(8,128)(2,1)}, bf16[384,2,512]{2,0,1:T(8,128)(2,1)S(1)}, u32[]{:S(2)}, u32[]{:S(2)}) collective-permute-start(bf16[384,2,512]{2,0,1:T(8,128)(2,1)} %collective-permute-done.11), channel_id=1, source_target_pairs={{0,240},{16,0},{32,16},{48,32},{64,48},{80,64},{96,80},{112,96},{1... | collective-permute-start | bytes 2359304 | tf_op jit(solution)/shard_map/ppermute | solution.py:28
  200.9 17.7 %collective-permute-start.14 = (bf16[384,2,512]{2,0,1:T(8,128)(2,1)}, bf16[384,2,512]{2,0,1:T(8,128)(2,1)S(1)}, u32[]{:S(2)}, u32[]{:S(2)}) collective-permute-start(bf16[384,2,512]{2,0,1:T(8,128)(2,1)} %collective-permute-done.12), channel_id=1, source_target_pairs={{0,16},{16,32},{32,48},{48,64},{64,80},{80,96},{96,112},{112,128},... | collective-permute-start | bytes 2359304 | tf_op jit(solution)/shard_map/ppermute | solution.py:19
  208.6 18.6 %collective-permute-start.15 = (bf16[384,2,512]{2,0,1:T(8,128)(2,1)S(1)}, bf16[384,2,512]{2,0,1:T(8,128)(2,1)S(1)}, u32[]{:S(2)}, u32[]{:S(2)}) collective-permute-start(bf16[384,2,512]{2,0,1:T(8,128)(2,1)S(1)} %collective-permute-done.13), channel_id=1, source_target_pairs={{0,240},{16,0},{32,16},{48,32},{64,48},{80,64},{96,80},{112,96},{1... | collective-permute-start | bytes 2359304 | tf_op jit(solution)/shard_map/ppermute | solution.py:28
  218.6 16.9 %collective-permute-start.16 = (bf16[384,2,512]{2,0,1:T(8,128)(2,1)S(1)}, bf16[384,2,512]{2,0,1:T(8,128)(2,1)S(1)}, u32[]{:S(2)}, u32[]{:S(2)}) collective-permute-start(bf16[384,2,512]{2,0,1:T(8,128)(2,1)S(1)} %collective-permute-done.14), channel_id=1, source_target_pairs={{0,16},{16,32},{32,48},{48,64},{64,80},{80,96},{96,112},{112,128},... | collective-permute-start | bytes 2359304 | tf_op jit(solution)/shard_map/ppermute | solution.py:19
  244.5 154.8 %reduce-scatter.5.cloned.1.call-start = ((), (), s32[]{:S(2)}) async-start(), calls=%async_computation.3 | async-start | bytes 10027008 | tf_op jit(solution)/shard_map/reduce_scatter | solution.py:100
Sparse Core Ops, SparseCore 0:
  244.6 80.0 reduce-scatter.2
  327.3 71.9 reduce-scatter.4
